TPU v7x, 32 devices: a whole 2x2x4 slice. The times are simulated.
32 devices in a mesh: group: 2 (over x), cell: 16 (over z, y, core).
Axes of the slice: x: 2, y: 2, z: 4, core: 2. Of those that a mesh axis runs over, the one named last changes fastest.
Arguments:
- cell_factor: bfloat16 [32768, 128], P(('group', 'cell')), parts along dimension 0, may hold values from -6 to 6
- sched_factor: bfloat16 [16384, 128], P('group'), parts along dimension 0, may hold values from -6 to 6
- core_matrix: float32 [256, 128], P('group'), parts along dimension 0, may hold values from -0.03125 to 0.03125
- rate_table: bfloat16 [64, 128], replicated, may hold values from 0.5 to 2
- cell_well: int32 [32768], P(('group', 'cell')), parts along dimension 0, may hold values from 0 to 63
- sched_profile: int32 [16384], P('group'), parts along dimension 0, may hold values from 0 to 127
Outputs:
- basis_cells: float32 [32768, 256], P(('group', 'cell')), parts along dimension 0
- basis_sched: float32 [16384, 256], P(('group', 'cell')), parts along dimension 0
- core_out: float32 [512, 256], P('group'), parts along dimension 0
There are 2 independent parts, one for each index of `group`. A program takes and returns all parts, laid end to end along the dimension named above; an argument that names none is the same for every part. Nothing has to cross between parts.
All inputs are finite; a program needn't handle non-finite values.
Results may differ from a plain program's by a relative error of at most 0.02.
Values may be sent and summed in bfloat16 or wider, within the bound.
A program may use at most 128 MiB of HBM per device.

v0:
```python
import functools

import jax
import jax.numpy as jnp
from jax import lax
from jax.experimental import pallas as pl
from jax.experimental.pallas import tpu as pltpu
from jax.sharding import PartitionSpec as P

TIME_STEP = 0.25
PANEL_SCALE = 8.0
HIGH = lax.Precision.HIGHEST
F32 = jnp.float32
BF16 = jnp.bfloat16
CHUNKS = 4
VMEM_LIMIT = 64 * 1000 * 1000


def dot(a, b, ca, cb, precision=None):
    return lax.dot_general(
        a, b, (((ca,), (cb,)), ((), ())), precision=precision, preferred_element_type=F32
    )


def bit_order(devices):
    bits = devices.bit_length() - 1
    return [b for b in (0, 1) if b < bits] + list(range(bits - 1, 1, -1))


def owner_of(place, devices):
    order = bit_order(devices)
    bits = len(order)
    total = 0
    for s, b in enumerate(order):
        total = total + ((place // (1 << (bits - 1 - s))) % 2) * (1 << b)
    return total


def tile_kernel(
    devices, k_scale,
    cell_ref, core_ref, rate_ref, well_ref, sched_ref, prof_ref,
    ly_ref, k_ref, gram_u_ref, gram_s_ref,
    tile, mix, rates, kacc, panel_t,
):
    step = pl.program_id(0)
    cells, width = cell_ref.shape
    block = sched_ref.shape[0]
    wells, profiles = rate_ref.shape

    @pl.when(step == 0)
    def _():
        mix[...] = dot(cell_ref[...].astype(F32), core_ref[...], 1, 0, HIGH).astype(BF16)
        hot = (lax.broadcasted_iota(jnp.int32, (wells, cells), 0) == well_ref[...]).astype(F32)
        picked = dot(hot.T.astype(BF16), rate_ref[...], 1, 0)
        rates[...] = (TIME_STEP * picked).astype(BF16)
        kacc[...] = jnp.zeros_like(kacc)
        gram_s_ref[...] = jnp.zeros_like(gram_s_ref)

    @pl.when(step < devices)
    def _():
        sched = sched_ref[...]
        rebuilt = dot(mix[...], sched, 1, 1)
        hot = (
            lax.broadcasted_iota(jnp.int32, (profiles, block), 0) == prof_ref[0]
        ).astype(F32).astype(BF16)
        inject = dot(rates[...], hot, 1, 0)
        state = (
            rebuilt * ((1.0 + TIME_STEP) - TIME_STEP * (rebuilt * rebuilt)) + inject
        ).astype(BF16)
        tile[step] = state
        kacc[...] += dot(state, sched, 1, 0)
        gram_s_ref[...] += dot(sched.astype(F32).T.astype(BF16), sched, 1, 0)

    @pl.when(step == devices - 1)
    def _():
        k = kacc[...] * k_scale
        k_ref[...] = k
        k_t = k.T
        cell_t = cell_ref[...].astype(F32).T
        both = jnp.concatenate([cell_t, k_t], axis=0)
        panel_t[...] = both.astype(BF16)
        gram_u_ref[...] = dot(both, both, 1, 1, HIGH)

    @pl.when(step >= devices)
    def _():
        owner = owner_of(step - devices, devices)
        ly_ref[0] = dot(panel_t[...], tile[owner], 1, 0).astype(BF16)


def comm_kernel(
    devices, l_scale,
    x_ref, gram_ref,
    ly_ref, gram_out, lg_out,
    *scratch,
):
    order = bit_order(devices)
    stages = len(order)
    recv = scratch[:stages]
    g_recv, g_acc, l_recv, l_acc, xs, xr, gs, gr, ls, lr = scratch[stages:]
    me = lax.axis_index("cell")
    rows = x_ref.shape[1] // CHUNKS
    digits = [(me // (1 << b)) % 2 for b in order]
    partners = [me + (1 - 2 * d) * (1 << b) for d, b in zip(digits, order)]

    barrier = pltpu.get_barrier_semaphore()
    for p in partners:
        pl.semaphore_signal(
            barrier, inc=1, device_id={"cell": p}, device_id_type=pl.DeviceIdType.MESH
        )
    pl.semaphore_wait(barrier, stages)

    def remote(src, dst, ssem, rsem, s):
        return pltpu.make_async_remote_copy(
            src_ref=src, dst_ref=dst, send_sem=ssem, recv_sem=rsem,
            device_id={"cell": partners[s]}, device_id_type=pl.DeviceIdType.MESH,
        )

    def big(s, c):
        half = devices >> (s + 1)
        cur = x_ref if s == 0 else recv[s - 1]
        part = pl.ds(c * rows, rows)
        return remote(
            cur.at[pl.ds((1 - digits[s]) * half, half), part],
            recv[s].at[:, part], xs.at[s, c], xr.at[s, c], s,
        )

    def small(s, buf, acc, ssem, rsem):
        return remote(acc.at[s], buf.at[s], ssem.at[s], rsem.at[s], s)

    def fold(s, c):
        half = devices >> (s + 1)
        cur = x_ref if s == 0 else recv[s - 1]
        part = pl.ds(c * rows, rows)
        if s == stages - 1:
            ly_ref[part] = (
                recv[s][0, part].astype(F32) + cur[digits[s], part].astype(F32)
            )
        else:
            def body(i, carry):
                recv[s][i, part] = (
                    recv[s][i, part].astype(F32)
                    + cur[digits[s] * half + i, part].astype(F32)
                ).astype(BF16)
                return carry
            lax.fori_loop(0, half, body, 0)

    g_acc[0] = gram_ref[...]
    small(0, g_recv, g_acc, gs, gr).start()
    for c in range(CHUNKS):
        big(0, c).start()
    for d in range(stages + CHUNKS - 1):
        for s in range(stages - 1, -1, -1):
            c = d - s
            if 0 <= c < CHUNKS:
                big(s, c).wait_recv()
                fold(s, c)
                if s + 1 < stages:
                    big(s + 1, c).start()
        if d < stages:
            small(d, g_recv, g_acc, gs, gr).wait_recv()
            total = g_acc[d] + g_recv[d]
            if d + 1 < stages:
                g_acc[d + 1] = total
                small(d + 1, g_recv, g_acc, gs, gr).start()
            else:
                gram_out[...] = total
    width = l_acc.shape[2]
    left = ly_ref[0:width]
    l_acc[0] = dot(ly_ref[...], left, 1, 1, HIGH)
    for s in range(stages):
        copy = small(s, l_recv, l_acc, ls, lr)
        copy.start()
        copy.wait_recv()
        total = l_acc[s] + l_recv[s]
        if s + 1 < stages:
            l_acc[s + 1] = total
        else:
            lg_out[...] = total
    for s in range(stages):
        for c in range(CHUNKS):
            big(s, c).wait_send()
        small(s, g_recv, g_acc, gs, gr).wait_send()
        small(s, l_recv, l_acc, ls, lr).wait_send()


def eliminate(w, pieces=4):
    n = w.shape[1]
    size = n // pieces
    for piece in range(pieces):
        low = piece * size
        count = n - low
        row_id = lax.broadcasted_iota(jnp.int32, (count, 1), 0) + low
        lane_id = lax.broadcasted_iota(jnp.int32, (1, n), 1)

        def body(t, carry):
            j = low + t
            here = lane_id == j
            for m in range(2):
                row = w[m, pl.ds(j, 1), :]
                col = jnp.sum(
                    jnp.where(here, w[m, low:n, 0:n], 0.0), axis=1, keepdims=True
                )
                pivot = jnp.sum(jnp.where(here, row[:, 0:n], 0.0), axis=1, keepdims=True)
                factor = jnp.where(row_id > j, col * (1.0 / pivot), 0.0)
                w[m, low:n, :] = w[m, low:n, :] - factor * row
            return carry

        lax.fori_loop(0, size, body, 0)


def inverse_pair(w, first, second):
    n = w.shape[1]
    eye = (
        lax.broadcasted_iota(jnp.int32, (n, n), 0) == lax.broadcasted_iota(jnp.int32, (n, n), 1)
    ).astype(F32)
    for m, a in enumerate((first, second)):
        w[m, :, 0:n] = a
        w[m, :, n : 2 * n] = eye
    eliminate(w)
    outs = []
    for m in range(2):
        diag = jnp.sum(w[m, :, 0:n] * eye, axis=1, keepdims=True)
        outs.append(w[m, :, n : 2 * n] * lax.rsqrt(diag))
    return outs


def finish_kernel(
    n_cells, n_sched, l_scale,
    gram_u_ref, gram_s_ref, lg_ref, cell_ref, k_ref, sched_ref, ly_ref,
    cells_ref, rows_ref, core_ref,
    w,
):
    n = gram_s_ref.shape[0]
    cc, ck, kk = gram_u_ref[0:n, 0:n], gram_u_ref[0:n, n:], gram_u_ref[n:, n:]
    sl = (ck.T) * (n_sched / n_cells)
    ll = lg_ref[0:n] * (l_scale * l_scale)
    yl = lg_ref[n:] * l_scale
    u11, v11 = inverse_pair(w, cc, gram_s_ref[...])
    xu = dot(u11, ck, 1, 0, HIGH)
    xv = dot(v11, sl, 1, 0, HIGH)
    u22, v22 = inverse_pair(w, kk - dot(xu.T, xu, 1, 0, HIGH), ll - dot(xv.T, xv, 1, 0, HIGH))
    u21 = -dot(u22, dot(xu.T, u11, 1, 0, HIGH), 1, 0, HIGH)
    v21 = -dot(v22, dot(xv.T, v11, 1, 0, HIGH), 1, 0, HIGH)

    size_u = float(n_cells) ** 0.5
    size_v = float(n_sched) ** 0.5
    cell = cell_ref[...].astype(F32)
    cells_ref[:, 0:n] = dot(cell, u11 * size_u, 1, 1, HIGH)
    cells_ref[:, n:] = dot(cell, u21 * size_u, 1, 1, HIGH) + dot(
        k_ref[...], u22 * size_u, 1, 1, HIGH
    )
    sched = sched_ref[...].astype(F32)
    l_rows = (ly_ref[0:n] * l_scale).T
    rows_ref[:, 0:n] = dot(sched, v11 * size_v, 1, 1, HIGH)
    rows_ref[:, n:] = dot(sched, v21 * size_v, 1, 1, HIGH) + dot(
        l_rows, v22 * size_v, 1, 1, HIGH
    )

    k_unscale = n_sched / PANEL_SCALE
    l_unscale = n_cells / PANEL_SCALE
    m11 = ck * k_unscale
    m12 = ll * l_unscale
    m21 = kk * k_unscale
    m22 = yl
    t11 = dot(u11, m11, 1, 0, HIGH)
    t12 = dot(u11, m12, 1, 0, HIGH)
    t21 = dot(u21, m11, 1, 0, HIGH) + dot(u22, m21, 1, 0, HIGH)
    t22 = dot(u21, m12, 1, 0, HIGH) + dot(u22, m22, 1, 0, HIGH)
    scale = n / (float(n_cells) * float(n_sched)) ** 0.5
    core_ref[0:n, 0:n] = scale * dot(t11, v11, 1, 1, HIGH)
    core_ref[n:, 0:n] = scale * dot(t21, v11, 1, 1, HIGH)
    core_ref[0:n, n:] = scale * (dot(t11, v21, 1, 1, HIGH) + dot(t12, v22, 1, 1, HIGH))
    core_ref[n:, n:] = scale * (dot(t21, v21, 1, 1, HIGH) + dot(t22, v22, 1, 1, HIGH))


def local(cell_factor, sched_factor, core_matrix, rate_table, cell_well, sched_profile):
    cells, width = cell_factor.shape
    n_sched = sched_factor.shape[0]
    devices = lax.axis_size("cell")
    n_cells = cells * devices
    block = n_sched // devices
    wells, profiles = rate_table.shape
    stages = devices.bit_length() - 1
    l_scale = PANEL_SCALE / n_cells
    full = lambda *shape: pl.BlockSpec(shape, lambda i: (0,) * len(shape))
    sds = jax.ShapeDtypeStruct

    ly_parts, k, gram_u, gram_s = pl.pallas_call(
        functools.partial(tile_kernel, devices, PANEL_SCALE / n_sched),
        grid=(2 * devices,),
        in_specs=[
            full(cells, width),
            full(width, width),
            full(wells, profiles),
            full(1, cells),
            pl.BlockSpec((block, width), lambda i: (jnp.minimum(i, devices - 1), 0)),
            pl.BlockSpec((1, 1, block), lambda i: (jnp.minimum(i, devices - 1), 0, 0)),
        ],
        out_specs=[
            pl.BlockSpec(
                (1, 2 * width, block), lambda i: (jnp.maximum(i - devices, 0), 0, 0)
            ),
            full(cells, width),
            full(2 * width, 2 * width),
            full(width, width),
        ],
        out_shape=[
            sds((devices, 2 * width, block), BF16),
            sds((cells, width), F32),
            sds((2 * width, 2 * width), F32),
            sds((width, width), F32),
        ],
        scratch_shapes=[
            pltpu.VMEM((devices, cells, block), BF16),
            pltpu.VMEM((cells, width), BF16),
            pltpu.VMEM((cells, profiles), BF16),
            pltpu.VMEM((cells, width), F32),
            pltpu.VMEM((2 * width, cells), BF16),
        ],
        compiler_params=pltpu.CompilerParams(
            dimension_semantics=("arbitrary",), vmem_limit_bytes=VMEM_LIMIT
        ),
    )(
        cell_factor, core_matrix, rate_table, cell_well.reshape(1, cells),
        sched_factor, sched_profile.reshape(devices, 1, block),
    )

    vmem = pl.BlockSpec(memory_space=pltpu.VMEM)
    dma = pltpu.SemaphoreType.DMA
    ly, gram_u, lg = pl.pallas_call(
        functools.partial(comm_kernel, devices, l_scale),
        in_specs=[vmem, vmem],
        out_specs=[vmem, vmem, vmem],
        out_shape=[
            sds((2 * width, block), F32),
            sds((2 * width, 2 * width), F32),
            sds((2 * width, width), F32),
        ],
        scratch_shapes=[
            pltpu.VMEM((devices >> (s + 1), 2 * width, block), BF16) for s in range(stages)
        ]
        + [
            pltpu.VMEM((stages, 2 * width, 2 * width), F32),
            pltpu.VMEM((stages, 2 * width, 2 * width), F32),
            pltpu.VMEM((stages, 2 * width, width), F32),
            pltpu.VMEM((stages, 2 * width, width), F32),
            dma((stages, CHUNKS)), dma((stages, CHUNKS)),
            dma((stages,)), dma((stages,)), dma((stages,)), dma((stages,)),
        ],
        compiler_params=pltpu.CompilerParams(
            collective_id=0, has_side_effects=True, vmem_limit_bytes=VMEM_LIMIT
        ),
    )(ly_parts, gram_u)

    row_start = lax.axis_index("cell") * block
    sched_rows = lax.dynamic_slice_in_dim(sched_factor, row_start, block, 0)
    return pl.pallas_call(
        functools.partial(finish_kernel, n_cells, n_sched, l_scale),
        in_specs=[vmem] * 7,
        out_specs=[vmem] * 3,
        out_shape=[
            sds((cells, 2 * width), F32),
            sds((block, 2 * width), F32),
            sds((2 * width, 2 * width), F32),
        ],
        scratch_shapes=[pltpu.VMEM((2, width, 2 * width), F32)],
        compiler_params=pltpu.CompilerParams(vmem_limit_bytes=VMEM_LIMIT),
    )(gram_u, gram_s, lg, cell_factor, k, sched_rows, ly)


def solution(mesh):
    return jax.shard_map(
        local,
        mesh=mesh,
        in_specs=(
            P(("group", "cell"), None),
            P("group", None),
            P("group", None),
            P(),
            P(("group", "cell")),
            P("group"),
        ),
        out_specs=(P(("group", "cell"), None), P(("group", "cell"), None), P("group", None)),
        check_vma=False,
    )
```

profile of v0, /device:TPU:0, one launch (start us, length us, event | category | flops | bytes accessed | tf_op | source)
XLA Modules:
  0.0 168.7 jit_solution(7722577321276957802)
XLA Ops:
  0.6 30.8 %shard_map.85 = (bf16[16,256,512]{2,1,0:T(8,128)(2,1)}, f32[1024,128]{1,0:T(8,128)}, f32[256,256]{1,0:T(8,128)}, f32[128,128]{1,0:T(8,128)}) custom-call(bf16[1024,128]{1,0:T(8,128)(2,1)} %cell_ref.3, f32[128,128]{1,0:T(8,128)} %core_ref.1, bf16[64,128]{1,0:T(8,128)(2,1)} %rate_ref.1, s32[1,1024]{1,0:T(1,128)} %bitcast.3, bf16[8192,128]{1,0:T(8,128)(2,1)} %sched_ref.1, ...), custom_call_target="tpu_custom_call" | custom-call | tf_op jit(solution)/shard_map/pallas_call | solution.py:288
  31.5 79.3 %shard_map.86 = (f32[256,512]{1,0:T(8,128)}, f32[256,256]{1,0:T(8,128)}, f32[256,128]{1,0:T(8,128)}) custom-call(bf16[16,256,512]{2,1,0:T(8,128)(2,1)} %get-tuple-element.10.x_ref, f32[256,256]{1,0:T(8,128)} %get-tuple-element.11.gram_ref), custom_call_target="tpu_custom_call" | custom-call | tf_op jit(solution)/shard_map/pallas_call | solution.py:330
  110.8 1.6 constant_dynamic-slice_fusion.sched_ref
  112.3 56.4 %shard_map.87 = (f32[1024,256]{1,0:T(8,128)}, f32[512,256]{1,0:T(8,128)}, f32[256,256]{1,0:T(8,128)}) custom-call(f32[256,256]{1,0:T(8,128)} %get-tuple-element.12.gram_u_ref, f32[128,128]{1,0:T(8,128)} %get-tuple-element.13.gram_s_ref, f32[256,128]{1,0:T(8,128)} %get-tuple-element.14.lg_ref, bf16[1024,128]{1,0:T(8,128)(2,1)} %cell_ref.3, ...), custom_call_target="tpu_custom_call" | custom-call | tf_op jit(solution)/shard_map/pallas_call | solution.py:357
where the time goes:
time: 169 us
  Pallas kernels  166 us (98%)
    pallas_call x1, Pallas kernels, local(): pl.pallas_call(functools.partial(comm_kernel, devices, l_scale), in_specs...  79.3 us
    pallas_call x1, Pallas kernels, local(): pl.pallas_call(functools.partial(finish_kernel, n_cells, n_sched, l_scale...  56.4 us
    pallas_call x1, Pallas kernels, local(): pl.pallas_call(functools.partial(tile_kernel, devices, PANEL_SCALE / n_sc...  30.8 us

commit v1 on v0

v1 whole, which is shorter than its diff:
```python
import functools

import jax
import jax.numpy as jnp
from jax import lax
from jax.experimental import pallas as pl
from jax.experimental.pallas import tpu as pltpu
from jax.sharding import PartitionSpec as P

TIME_STEP = 0.25
PANEL_SCALE = 8.0
HIGH = lax.Precision.HIGHEST
F32 = jnp.float32
BF16 = jnp.bfloat16
CHUNKS = 4
BLOCK = 16
VMEM_LIMIT = 64 * 1000 * 1000


def dot(a, b, ca, cb, precision=None):
    return lax.dot_general(
        a, b, (((ca,), (cb,)), ((), ())), precision=precision, preferred_element_type=F32
    )


def bit_order(devices):
    bits = devices.bit_length() - 1
    return [b for b in (0, 1) if b < bits] + list(range(bits - 1, 1, -1))


def owner_of(place, devices):
    order = bit_order(devices)
    bits = len(order)
    total = 0
    for s, b in enumerate(order):
        total = total + ((place // (1 << (bits - 1 - s))) % 2) * (1 << b)
    return total


def tile_kernel(
    devices, k_scale,
    cell_ref, core_ref, rate_ref, well_ref, sched_ref, prof_ref,
    ly_ref, k_ref, gram_u_ref, gram_s_ref,
    tile, mix, rates, kacc, panel_t,
):
    step = pl.program_id(0)
    cells, width = cell_ref.shape
    block = sched_ref.shape[0]
    wells, profiles = rate_ref.shape

    @pl.when(step == 0)
    def _():
        mix[...] = dot(cell_ref[...].astype(F32), core_ref[...], 1, 0, HIGH).astype(BF16)
        hot = (lax.broadcasted_iota(jnp.int32, (wells, cells), 0) == well_ref[...]).astype(F32)
        picked = dot(hot.T.astype(BF16), rate_ref[...], 1, 0)
        rates[...] = (TIME_STEP * picked).astype(BF16)
        kacc[...] = jnp.zeros_like(kacc)
        gram_s_ref[...] = jnp.zeros_like(gram_s_ref)

    @pl.when(step < devices)
    def _():
        sched = sched_ref[...]
        rebuilt = dot(mix[...], sched, 1, 1)
        hot = (
            lax.broadcasted_iota(jnp.int32, (profiles, block), 0) == prof_ref[0]
        ).astype(F32).astype(BF16)
        inject = dot(rates[...], hot, 1, 0)
        state = (
            rebuilt * ((1.0 + TIME_STEP) - TIME_STEP * (rebuilt * rebuilt)) + inject
        ).astype(BF16)
        tile[step] = state
        kacc[...] += dot(state, sched, 1, 0)
        gram_s_ref[...] += dot(sched.astype(F32).T.astype(BF16), sched, 1, 0)

    @pl.when(step == devices - 1)
    def _():
        k = kacc[...] * k_scale
        k_ref[...] = k
        k_t = k.T
        cell_t = cell_ref[...].astype(F32).T
        both = jnp.concatenate([cell_t, k_t], axis=0)
        panel_t[...] = both.astype(BF16)
        gram_u_ref[...] = dot(both, both, 1, 1, HIGH)

    @pl.when(step >= devices)
    def _():
        owner = owner_of(step - devices, devices)
        ly_ref[0] = dot(panel_t[...], tile[owner], 1, 0).astype(BF16)


def eliminate(w, m, low, high):
    n = w.shape[1]
    lane = lax.broadcasted_iota(jnp.int32, (1, n), 1)
    rid = lax.broadcasted_iota(jnp.int32, (BLOCK, 1), 0)

    def body(b, carry):
        base = pl.multiple_of(b * BLOCK, BLOCK)
        rows = w[m, pl.ds(base, BLOCK), :]
        cols = [
            jnp.sum(jnp.where(lane == base + t, rows[:, 0:n], 0.0), axis=1, keepdims=True)
            for t in range(BLOCK)
        ]
        inverse = jnp.zeros((BLOCK, 1), F32)
        for t in range(BLOCK):
            recip = 1.0 / cols[t][t : t + 1, :]
            inverse = jnp.where(rid == t, recip, inverse)
            factor = jnp.where(rid > t, cols[t] * recip, 0.0)
            for later in range(t + 1, BLOCK):
                cols[later] = cols[later] - factor * cols[later][t : t + 1, :]
            rows = rows - factor * rows[t : t + 1, :]
        w[m, pl.ds(base, BLOCK), :] = rows
        left = jnp.where(lane >= base + BLOCK, rows[:, 0:n] * inverse, 0.0)
        w[m] = w[m] - dot(left, rows, 0, 0, HIGH)
        return carry

    lax.fori_loop(low, high, body, 0)


def identity(n):
    return (
        lax.broadcasted_iota(jnp.int32, (n, n), 0) == lax.broadcasted_iota(jnp.int32, (n, n), 1)
    ).astype(F32)


def load(w, m, a):
    n = w.shape[1]
    w[m, :, 0:n] = a
    w[m, :, n : 2 * n] = identity(n)


def factor_inverse(w, m):
    n = w.shape[1]
    diag = jnp.sum(w[m, :, 0:n] * identity(n), axis=1, keepdims=True)
    return w[m, :, n : 2 * n] * lax.rsqrt(diag)


def comm_kernel(
    devices, n_cells, n_sched,
    x_ref, gram_ref, gram_s_ref, cell_ref, k_ref, sched_ref,
    cells_ref, rows_ref, core_ref,
    *scratch,
):
    order = bit_order(devices)
    stages = len(order)
    recv = scratch[:stages]
    (
        ly, g_recv, g_acc, l_recv, l_acc, y_recv, y_acc, w, inv, sched_own,
        xs, xr, gs, gr, ls, lr, ys, yr, own_sem,
    ) = scratch[stages:]
    n = gram_s_ref.shape[0]
    l_scale = PANEL_SCALE / n_cells
    me = lax.axis_index("cell")
    block = sched_own.shape[0]
    rows = x_ref.shape[1] // CHUNKS
    digits = [(me // (1 << b)) % 2 for b in order]
    partners = [me + (1 - 2 * d) * (1 << b) for d, b in zip(digits, order)]

    own = pltpu.make_async_copy(
        sched_ref.at[pl.ds(pl.multiple_of(me * block, block), block)], sched_own, own_sem
    )
    own.start()
    barrier = pltpu.get_barrier_semaphore()
    for p in partners:
        pl.semaphore_signal(
            barrier, inc=1, device_id={"cell": p}, device_id_type=pl.DeviceIdType.MESH
        )
    pl.semaphore_wait(barrier, stages)

    def remote(src, dst, ssem, rsem, s):
        return pltpu.make_async_remote_copy(
            src_ref=src, dst_ref=dst, send_sem=ssem, recv_sem=rsem,
            device_id={"cell": partners[s]}, device_id_type=pl.DeviceIdType.MESH,
        )

    def big(s, c):
        half = devices >> (s + 1)
        cur = x_ref if s == 0 else recv[s - 1]
        part = pl.ds(c * rows, rows)
        return remote(
            cur.at[pl.ds((1 - digits[s]) * half, half), part],
            recv[s].at[:, part], xs.at[s, c], xr.at[s, c], s,
        )

    def fold(s, c):
        half = devices >> (s + 1)
        cur = x_ref if s == 0 else recv[s - 1]
        part = pl.ds(c * rows, rows)
        if s == stages - 1:
            ly[part] = recv[s][0, part].astype(F32) + cur[digits[s], part].astype(F32)
        else:
            def body(i, carry):
                recv[s][i, part] = (
                    recv[s][i, part].astype(F32)
                    + cur[digits[s] * half + i, part].astype(F32)
                ).astype(BF16)
                return carry
            lax.fori_loop(0, half, body, 0)

    small = {"g": (g_recv, g_acc, gs, gr), "l": (l_recv, l_acc, ls, lr), "y": (y_recv, y_acc, ys, yr)}

    def hop(name, s):
        buf, acc, ssem, rsem = small[name]
        return remote(acc.at[s], buf.at[s], ssem.at[s], rsem.at[s], s)

    def begin(name, value):
        small[name][1][0] = value
        hop(name, 0).start()

    def advance(name, s):
        buf, acc, _, _ = small[name]
        hop(name, s).wait_recv()
        acc[s + 1] = acc[s] + buf[s]
        if s + 1 < stages:
            hop(name, s + 1).start()

    begin("g", jnp.concatenate([gram_ref[0:n, 0:n], gram_ref[0:n, n:], gram_ref[n:, n:]], axis=0))
    for c in range(CHUNKS):
        big(0, c).start()

    pieces = n // BLOCK
    cut = pieces // 2
    g = lambda i: g_acc[stages, i * n : (i + 1) * n]
    size_u = float(n_cells) ** 0.5
    size_v = float(n_sched) ** 0.5

    def schur(slot, corner, side, square):
        x = dot(inv[slot], side, 1, 0, HIGH)
        inv[slot + 1] = dot(x, inv[slot], 0, 0, HIGH)
        load(w, corner, square - dot(x, x, 0, 0, HIGH))

    def work_v_first():
        load(w, 1, gram_s_ref[...])
        eliminate(w, 1, 0, cut)

    def work_v_second():
        eliminate(w, 1, cut, pieces)
        inv[3] = factor_inverse(w, 1)

    def work_u_first():
        load(w, 0, g(0))
        eliminate(w, 0, 0, pieces)
        inv[0] = factor_inverse(w, 0)

    def work_u_second():
        schur(0, 0, g(1), g(2))
        eliminate(w, 0, 0, cut)

    def work_u_third():
        eliminate(w, 0, cut, pieces)
        inv[2] = factor_inverse(w, 0)
        inv[1] = -dot(inv[2], inv[1], 1, 0, HIGH)

    def work_cells():
        cell = cell_ref[...].astype(F32)
        cells_ref[:, 0:n] = dot(cell, inv[0] * size_u, 1, 1, HIGH)
        cells_ref[:, n:] = dot(cell, inv[1] * size_u, 1, 1, HIGH) + dot(
            k_ref[...], inv[2] * size_u, 1, 1, HIGH
        )

    jobs = [work_v_first, work_v_second, work_u_first, work_u_second, work_u_third, work_cells]
    done = 0
    for d in range(stages + CHUNKS - 1):
        for s in range(stages - 1, -1, -1):
            c = d - s
            if 0 <= c < CHUNKS:
                big(s, c).wait_recv()
                fold(s, c)
                if s + 1 < stages:
                    big(s + 1, c).start()
        if d < stages:
            advance("g", d)
        if d < stages + CHUNKS - 2 and done < len(jobs) and (done < 2 or d >= stages - 1):
            jobs[done]()
            done += 1

    left = ly[0:n]
    begin("l", dot(left, left, 1, 1, HIGH))
    begin("y", dot(ly[n : 2 * n], left, 1, 1, HIGH))
    for job in jobs[done : done + 1]:
        job()
    for s in range(stages):
        advance("l", s)
        for job in jobs[done + 1 + s : done + 2 + s]:
            job()
    ll = l_acc[stages] * (l_scale * l_scale)
    ck = g(1)
    schur(3, 1, ck.T * (n_sched / n_cells), ll)
    for s in range(stages):
        advance("y", s)
        eliminate(w, 1, pieces * s // stages, pieces * (s + 1) // stages)
    inv[5] = factor_inverse(w, 1)
    inv[4] = -dot(inv[5], inv[4], 1, 0, HIGH)
    yl = y_acc[stages] * l_scale
    u11, u21, u22, v11, v21, v22 = [inv[i] for i in range(6)]

    own.wait()
    sched = sched_own[...].astype(F32)
    l_rows = (left * l_scale).T
    rows_ref[:, 0:n] = dot(sched, v11 * size_v, 1, 1, HIGH)
    rows_ref[:, n:] = dot(sched, v21 * size_v, 1, 1, HIGH) + dot(
        l_rows, v22 * size_v, 1, 1, HIGH
    )

    k_unscale = n_sched / PANEL_SCALE
    m11 = ck * k_unscale
    m12 = ll * (1.0 / l_scale)
    m21 = g(2) * k_unscale
    t11 = dot(u11, m11, 1, 0, HIGH)
    t12 = dot(u11, m12, 1, 0, HIGH)
    t21 = dot(u21, m11, 1, 0, HIGH) + dot(u22, m21, 1, 0, HIGH)
    t22 = dot(u21, m12, 1, 0, HIGH) + dot(u22, yl, 1, 0, HIGH)
    scale = n / (float(n_cells) * float(n_sched)) ** 0.5
    core_ref[0:n, 0:n] = scale * dot(t11, v11, 1, 1, HIGH)
    core_ref[n:, 0:n] = scale * dot(t21, v11, 1, 1, HIGH)
    core_ref[0:n, n:] = scale * (dot(t11, v21, 1, 1, HIGH) + dot(t12, v22, 1, 1, HIGH))
    core_ref[n:, n:] = scale * (dot(t21, v21, 1, 1, HIGH) + dot(t22, v22, 1, 1, HIGH))
    for s in range(stages):
        for c in range(CHUNKS):
            big(s, c).wait_send()
        for name in small:
            hop(name, s).wait_send()


def local(cell_factor, sched_factor, core_matrix, rate_table, cell_well, sched_profile):
    cells, width = cell_factor.shape
    n_sched = sched_factor.shape[0]
    devices = lax.axis_size("cell")
    n_cells = cells * devices
    block = n_sched // devices
    wells, profiles = rate_table.shape
    stages = devices.bit_length() - 1
    full = lambda *shape: pl.BlockSpec(shape, lambda i: (0,) * len(shape))
    sds = jax.ShapeDtypeStruct

    ly_parts, k, gram_u, gram_s = pl.pallas_call(
        functools.partial(tile_kernel, devices, PANEL_SCALE / n_sched),
        grid=(2 * devices,),
        in_specs=[
            full(cells, width),
            full(width, width),
            full(wells, profiles),
            full(1, cells),
            pl.BlockSpec((block, width), lambda i: (jnp.minimum(i, devices - 1), 0)),
            pl.BlockSpec((1, 1, block), lambda i: (jnp.minimum(i, devices - 1), 0, 0)),
        ],
        out_specs=[
            pl.BlockSpec(
                (1, 2 * width, block), lambda i: (jnp.maximum(i - devices, 0), 0, 0)
            ),
            full(cells, width),
            full(2 * width, 2 * width),
            full(width, width),
        ],
        out_shape=[
            sds((devices, 2 * width, block), BF16),
            sds((cells, width), F32),
            sds((2 * width, 2 * width), F32),
            sds((width, width), F32),
        ],
        scratch_shapes=[
            pltpu.VMEM((devices, cells, block), BF16),
            pltpu.VMEM((cells, width), BF16),
            pltpu.VMEM((cells, profiles), BF16),
            pltpu.VMEM((cells, width), F32),
            pltpu.VMEM((2 * width, cells), BF16),
        ],
        compiler_params=pltpu.CompilerParams(
            dimension_semantics=("arbitrary",), vmem_limit_bytes=VMEM_LIMIT
        ),
    )(
        cell_factor, core_matrix, rate_table, cell_well.reshape(1, cells),
        sched_factor, sched_profile.reshape(devices, 1, block),
    )

    vmem = pl.BlockSpec(memory_space=pltpu.VMEM)
    dma = pltpu.SemaphoreType.DMA
    rest = pl.BlockSpec(memory_space=pl.ANY)
    return pl.pallas_call(
        functools.partial(comm_kernel, devices, n_cells, n_sched),
        in_specs=[vmem] * 5 + [rest],
        out_specs=[vmem] * 3,
        out_shape=[
            sds((cells, 2 * width), F32),
            sds((block, 2 * width), F32),
            sds((2 * width, 2 * width), F32),
        ],
        scratch_shapes=[
            pltpu.VMEM((devices >> (s + 1), 2 * width, block), BF16) for s in range(stages)
        ]
        + [
            pltpu.VMEM((2 * width, block), F32),
            pltpu.VMEM((stages, 3 * width, width), F32),
            pltpu.VMEM((stages + 1, 3 * width, width), F32),
            pltpu.VMEM((stages, width, width), F32),
            pltpu.VMEM((stages + 1, width, width), F32),
            pltpu.VMEM((stages, width, width), F32),
            pltpu.VMEM((stages + 1, width, width), F32),
            pltpu.VMEM((2, width, 2 * width), F32),
            pltpu.VMEM((6, width, width), F32),
            pltpu.VMEM((block, width), BF16),
            dma((stages, CHUNKS)), dma((stages, CHUNKS)),
        ]
        + [dma((stages,))] * 6
        + [dma],
        compiler_params=pltpu.CompilerParams(
            collective_id=0, has_side_effects=True, vmem_limit_bytes=VMEM_LIMIT
        ),
    )(ly_parts, gram_u, gram_s, cell_factor, k, sched_factor)


def solution(mesh):
    return jax.shard_map(
        local,
        mesh=mesh,
        in_specs=(
            P(("group", "cell"), None),
            P("group", None),
            P("group", None),
            P(),
            P(("group", "cell")),
            P("group"),
        ),
        out_specs=(P(("group", "cell"), None), P(("group", "cell"), None), P("group", None)),
        check_vma=False,
    )
```

time: 169 us -> 126 us (0.75)
  Pallas kernels: 166 us -> 119 us
  local copies, waits for them, and re-layouts: 1.55 us -> 5.8 us
    pallas_call x2 -> x1, Pallas kernels: 136 us -> 88 us  [local(): pl.pallas_call(functools.partial(comm_kernel, devices, n_cells, n_sched),...]
    unnamed x0 -> x3, local copies, waits for them, and re-layouts: none -> 5.8 us
where the time goes in v1:
time: 126 us; the launch traced here: 125 us
  Pallas kernels  119 us (94%)
  local copies, waits for them, and re-layouts  5.8 us (5%)
    pallas_call x1, Pallas kernels, local(): pl.pallas_call(functools.partial(comm_kernel, devices, n_cells, n_sched),...  88 us
    pallas_call x1, Pallas kernels, local(): pl.pallas_call(functools.partial(tile_kernel, devices, PANEL_SCALE / n_sc...  30.8 us
    unnamed x3, local copies, waits for them, and re-layouts  5.8 us

profile of v1, /device:TPU:0, one launch (start us, length us, event | category | flops | bytes accessed | tf_op | source)
XLA Modules:
  0.0 125.3 jit_solution(17226011970118899104)
XLA Ops:
  0.6 30.8 %shard_map.85 = (bf16[16,256,512]{2,1,0:T(8,128)(2,1)}, f32[1024,128]{1,0:T(8,128)}, f32[256,256]{1,0:T(8,128)}, f32[128,128]{1,0:T(8,128)}) custom-call(bf16[1024,128]{1,0:T(8,128)(2,1)} %cell_ref.3, f32[128,128]{1,0:T(8,128)} %core_ref.1, bf16[64,128]{1,0:T(8,128)(2,1)} %rate_ref.1, s32[1,1024]{1,0:T(1,128)} %bitcast.3, bf16[8192,128]{1,0:T(8,128)(2,1)} %sched_ref.3, ...), custom_call_target="tpu_custom_call" | custom-call | tf_op jit(solution)/shard_map/pallas_call | solution.py:335
  31.5 88.0 %shard_map.86 = (f32[1024,256]{1,0:T(8,128)}, f32[512,256]{1,0:T(8,128)}, f32[256,256]{1,0:T(8,128)}) custom-call(bf16[16,256,512]{2,1,0:T(8,128)(2,1)} %get-tuple-element.7.x_ref, f32[256,256]{1,0:T(8,128)} %get-tuple-element.8.gram_ref, f32[128,128]{1,0:T(8,128)} %get-tuple-element.9.gram_s_ref, bf16[1024,128]{1,0:T(8,128)(2,1)} %cell_ref.3, ...), custom_call_target="tpu_custom_call" | custom-call | tf_op jit(solution)/shard_map/pallas_call | solution.py:378
  119.5 2.3 %copy.12 = f32[1024,256]{1,0:T(8,128)} copy(f32[1024,256]{1,0:T(8,128)} %get-tuple-element.14) | data formatting | bytes 2097152
  121.8 1.9 %copy.13 = f32[512,256]{1,0:T(8,128)} copy(f32[512,256]{1,0:T(8,128)} %get-tuple-element.15) | data formatting | bytes 1048576
  123.6 1.7 %copy.14 = f32[256,256]{1,0:T(8,128)} copy(f32[256,256]{1,0:T(8,128)} %get-tuple-element.16) | data formatting | bytes 524288

commit v2 on v1

--- a/solution.py
+++ b/solution.py
@@ -35,57 +35,6 @@
     for s, b in enumerate(order):
         total = total + ((place // (1 << (bits - 1 - s))) % 2) * (1 << b)
     return total
-
-
-def tile_kernel(
-    devices, k_scale,
-    cell_ref, core_ref, rate_ref, well_ref, sched_ref, prof_ref,
-    ly_ref, k_ref, gram_u_ref, gram_s_ref,
-    tile, mix, rates, kacc, panel_t,
-):
-    step = pl.program_id(0)
-    cells, width = cell_ref.shape
-    block = sched_ref.shape[0]
-    wells, profiles = rate_ref.shape
-
-    @pl.when(step == 0)
-    def _():
-        mix[...] = dot(cell_ref[...].astype(F32), core_ref[...], 1, 0, HIGH).astype(BF16)
-        hot = (lax.broadcasted_iota(jnp.int32, (wells, cells), 0) == well_ref[...]).astype(F32)
-        picked = dot(hot.T.astype(BF16), rate_ref[...], 1, 0)
-        rates[...] = (TIME_STEP * picked).astype(BF16)
-        kacc[...] = jnp.zeros_like(kacc)
-        gram_s_ref[...] = jnp.zeros_like(gram_s_ref)
-
-    @pl.when(step < devices)
-    def _():
-        sched = sched_ref[...]
-        rebuilt = dot(mix[...], sched, 1, 1)
-        hot = (
-            lax.broadcasted_iota(jnp.int32, (profiles, block), 0) == prof_ref[0]
-        ).astype(F32).astype(BF16)
-        inject = dot(rates[...], hot, 1, 0)
-        state = (
-            rebuilt * ((1.0 + TIME_STEP) - TIME_STEP * (rebuilt * rebuilt)) + inject
-        ).astype(BF16)
-        tile[step] = state
-        kacc[...] += dot(state, sched, 1, 0)
-        gram_s_ref[...] += dot(sched.astype(F32).T.astype(BF16), sched, 1, 0)
-
-    @pl.when(step == devices - 1)
-    def _():
-        k = kacc[...] * k_scale
-        k_ref[...] = k
-        k_t = k.T
-        cell_t = cell_ref[...].astype(F32).T
-        both = jnp.concatenate([cell_t, k_t], axis=0)
-        panel_t[...] = both.astype(BF16)
-        gram_u_ref[...] = dot(both, both, 1, 1, HIGH)
-
-    @pl.when(step >= devices)
-    def _():
-        owner = owner_of(step - devices, devices)
-        ly_ref[0] = dot(panel_t[...], tile[owner], 1, 0).astype(BF16)
 
 
 def eliminate(w, m, low, high):
@@ -136,7 +85,7 @@
 
 def comm_kernel(
     devices, n_cells, n_sched,
-    x_ref, gram_ref, gram_s_ref, cell_ref, k_ref, sched_ref,
+    cell_ref, core_matrix_ref, rate_ref, well_ref, sched_ref, prof_ref,
     cells_ref, rows_ref, core_ref,
     *scratch,
 ):
@@ -144,21 +93,19 @@
     stages = len(order)
     recv = scratch[:stages]
     (
-        ly, g_recv, g_acc, l_recv, l_acc, y_recv, y_acc, w, inv, sched_own,
-        xs, xr, gs, gr, ls, lr, ys, yr, own_sem,
+        ly, c_recv, c_acc, g_recv, g_acc, l_recv, l_acc, y_recv, y_acc, w, inv,
+        x_ref, tile, mix, rates, k_ref, panel_t, gram_s,
+        xs0, xr0, xs, xr, cs, cr, gs, gr, ls, lr, ys, yr,
     ) = scratch[stages:]
-    n = gram_s_ref.shape[0]
+    cells, n = cell_ref.shape
+    block = sched_ref.shape[1]
+    wells, profiles = rate_ref.shape
     l_scale = PANEL_SCALE / n_cells
     me = lax.axis_index("cell")
-    block = sched_own.shape[0]
     rows = x_ref.shape[1] // CHUNKS
     digits = [(me // (1 << b)) % 2 for b in order]
     partners = [me + (1 - 2 * d) * (1 << b) for d, b in zip(digits, order)]
 
-    own = pltpu.make_async_copy(
-        sched_ref.at[pl.ds(pl.multiple_of(me * block, block), block)], sched_own, own_sem
-    )
-    own.start()
     barrier = pltpu.get_barrier_semaphore()
     for p in partners:
         pl.semaphore_signal(
@@ -196,7 +143,7 @@
                 return carry
             lax.fori_loop(0, half, body, 0)
 
-    small = {"g": (g_recv, g_acc, gs, gr), "l": (l_recv, l_acc, ls, lr), "y": (y_recv, y_acc, ys, yr)}
+    small = {"c": (c_recv, c_acc, cs, cr), "g": (g_recv, g_acc, gs, gr), "l": (l_recv, l_acc, ls, lr), "y": (y_recv, y_acc, ys, yr)}
 
     def hop(name, s):
         buf, acc, ssem, rsem = small[name]
@@ -213,13 +160,69 @@
         if s + 1 < stages:
             hop(name, s + 1).start()
 
-    begin("g", jnp.concatenate([gram_ref[0:n, 0:n], gram_ref[0:n, n:], gram_ref[n:, n:]], axis=0))
+    mix[...] = dot(cell_ref[...].astype(F32), core_matrix_ref[...], 1, 0, HIGH).astype(BF16)
+    hot_well = (lax.broadcasted_iota(jnp.int32, (wells, cells), 0) == well_ref[...]).astype(F32)
+    rates[...] = (TIME_STEP * dot(hot_well.T.astype(BF16), rate_ref[...], 1, 0)).astype(BF16)
+    cell_t = cell_ref[...].astype(F32).T
+    panel_t[0:n] = cell_t.astype(BF16)
+    begin("c", dot(panel_t[0:n], cell_ref[...], 1, 0))
+    k_ref[...] = jnp.zeros_like(k_ref)
+    gram_s[...] = jnp.zeros_like(gram_s)
+
+    def build(i, carry):
+        sched = sched_ref[i]
+        rebuilt = dot(mix[...], sched, 1, 1)
+        hot = (
+            lax.broadcasted_iota(jnp.int32, (profiles, block), 0) == prof_ref[i]
+        ).astype(F32).astype(BF16)
+        inject = dot(rates[...], hot, 1, 0)
+        state = (
+            rebuilt * ((1.0 + TIME_STEP) - TIME_STEP * (rebuilt * rebuilt)) + inject
+        ).astype(BF16)
+        tile[i] = state
+        k_ref[...] += dot(state, sched, 1, 0)
+        gram_s[...] += dot(sched.astype(F32).T.astype(BF16), sched, 1, 0)
+        return carry
+
+    for s in range(stages):
+        lax.fori_loop(devices * s // stages, devices * (s + 1) // stages, build, 0)
+        advance("c", s)
+
+    k_ref[...] = k_ref[...] * (PANEL_SCALE / n_sched)
+    k_t = k_ref[...].T
+    panel_t[n : 2 * n] = k_t.astype(BF16)
+    both = jnp.concatenate([cell_ref[...].astype(F32).T, k_t], axis=0)
+    begin("g", dot(both, k_t, 1, 1, HIGH))
+
+    half0 = devices // 2
+    group = half0 // 2
+
+    def project(i, carry):
+        x_ref[i] = dot(panel_t[...], tile[owner_of(i, devices)], 1, 0).astype(BF16)
+        return carry
+
+    def first(i):
+        return remote(
+            x_ref.at[(1 - digits[0]) * half0 + i], recv[0].at[i], xs0.at[i], xr0.at[i], 0
+        )
+
+    for part in range(2):
+        base = (1 - digits[0]) * half0 + part * group
+        lax.fori_loop(base, base + group, project, 0)
+        for i in range(part * group, (part + 1) * group):
+            first(i).start()
+    advance("g", 0)
+    lax.fori_loop(digits[0] * half0, digits[0] * half0 + half0, project, 0)
+    for i in range(half0):
+        first(i).wait_recv()
     for c in range(CHUNKS):
-        big(0, c).start()
+        fold(0, c)
+        big(1, c).start()
+    advance("g", 1)
 
     pieces = n // BLOCK
     cut = pieces // 2
-    g = lambda i: g_acc[stages, i * n : (i + 1) * n]
+    g = lambda i: g_acc[stages, (i - 1) * n : i * n] if i else c_acc[stages]
     size_u = float(n_cells) ** 0.5
     size_v = float(n_sched) ** 0.5
 
@@ -229,7 +232,7 @@
         load(w, corner, square - dot(x, x, 0, 0, HIGH))
 
     def work_v_first():
-        load(w, 1, gram_s_ref[...])
+        load(w, 1, gram_s[...])
         eliminate(w, 1, 0, cut)
 
     def work_v_second():
@@ -259,17 +262,17 @@
 
     jobs = [work_v_first, work_v_second, work_u_first, work_u_second, work_u_third, work_cells]
     done = 0
-    for d in range(stages + CHUNKS - 1):
-        for s in range(stages - 1, -1, -1):
-            c = d - s
+    for d in range(stages + CHUNKS - 2):
+        for s in range(stages - 1, 0, -1):
+            c = d - s + 1
             if 0 <= c < CHUNKS:
                 big(s, c).wait_recv()
                 fold(s, c)
                 if s + 1 < stages:
                     big(s + 1, c).start()
-        if d < stages:
-            advance("g", d)
-        if d < stages + CHUNKS - 2 and done < len(jobs) and (done < 2 or d >= stages - 1):
+        if d + 2 < stages:
+            advance("g", d + 2)
+        if done < len(jobs) and d < stages + CHUNKS - 3 and (done < 3 or d + 3 >= stages):
             jobs[done]()
             done += 1
 
@@ -293,8 +296,7 @@
     yl = y_acc[stages] * l_scale
     u11, u21, u22, v11, v21, v22 = [inv[i] for i in range(6)]
 
-    own.wait()
-    sched = sched_own[...].astype(F32)
+    sched = sched_ref[me].astype(F32)
     l_rows = (left * l_scale).T
     rows_ref[:, 0:n] = dot(sched, v11 * size_v, 1, 1, HIGH)
     rows_ref[:, n:] = dot(sched, v21 * size_v, 1, 1, HIGH) + dot(
@@ -314,9 +316,12 @@
     core_ref[n:, 0:n] = scale * dot(t21, v11, 1, 1, HIGH)
     core_ref[0:n, n:] = scale * (dot(t11, v21, 1, 1, HIGH) + dot(t12, v22, 1, 1, HIGH))
     core_ref[n:, n:] = scale * (dot(t21, v21, 1, 1, HIGH) + dot(t22, v22, 1, 1, HIGH))
+    for i in range(half0):
+        first(i).wait_send()
     for s in range(stages):
         for c in range(CHUNKS):
-            big(s, c).wait_send()
+            if s:
+                big(s, c).wait_send()
         for name in small:
             hop(name, s).wait_send()
 
@@ -329,55 +334,12 @@
     block = n_sched // devices
     wells, profiles = rate_table.shape
     stages = devices.bit_length() - 1
-    full = lambda *shape: pl.BlockSpec(shape, lambda i: (0,) * len(shape))
     sds = jax.ShapeDtypeStruct
-
-    ly_parts, k, gram_u, gram_s = pl.pallas_call(
-        functools.partial(tile_kernel, devices, PANEL_SCALE / n_sched),
-        grid=(2 * devices,),
-        in_specs=[
-            full(cells, width),
-            full(width, width),
-            full(wells, profiles),
-            full(1, cells),
-            pl.BlockSpec((block, width), lambda i: (jnp.minimum(i, devices - 1), 0)),
-            pl.BlockSpec((1, 1, block), lambda i: (jnp.minimum(i, devices - 1), 0, 0)),
-        ],
-        out_specs=[
-            pl.BlockSpec(
-                (1, 2 * width, block), lambda i: (jnp.maximum(i - devices, 0), 0, 0)
-            ),
-            full(cells, width),
-            full(2 * width, 2 * width),
-            full(width, width),
-        ],
-        out_shape=[
-            sds((devices, 2 * width, block), BF16),
-            sds((cells, width), F32),
-            sds((2 * width, 2 * width), F32),
-            sds((width, width), F32),
-        ],
-        scratch_shapes=[
-            pltpu.VMEM((devices, cells, block), BF16),
-            pltpu.VMEM((cells, width), BF16),
-            pltpu.VMEM((cells, profiles), BF16),
-            pltpu.VMEM((cells, width), F32),
-            pltpu.VMEM((2 * width, cells), BF16),
-        ],
-        compiler_params=pltpu.CompilerParams(
-            dimension_semantics=("arbitrary",), vmem_limit_bytes=VMEM_LIMIT
-        ),
-    )(
-        cell_factor, core_matrix, rate_table, cell_well.reshape(1, cells),
-        sched_factor, sched_profile.reshape(devices, 1, block),
-    )
-
     vmem = pl.BlockSpec(memory_space=pltpu.VMEM)
     dma = pltpu.SemaphoreType.DMA
-    rest = pl.BlockSpec(memory_space=pl.ANY)
     return pl.pallas_call(
         functools.partial(comm_kernel, devices, n_cells, n_sched),
-        in_specs=[vmem] * 5 + [rest],
+        in_specs=[vmem] * 6,
         out_specs=[vmem] * 3,
         out_shape=[
             sds((cells, 2 * width), F32),
@@ -389,23 +351,35 @@
         ]
         + [
             pltpu.VMEM((2 * width, block), F32),
-            pltpu.VMEM((stages, 3 * width, width), F32),
-            pltpu.VMEM((stages + 1, 3 * width, width), F32),
+            pltpu.VMEM((stages, width, width), F32),
+            pltpu.VMEM((stages + 1, width, width), F32),
+            pltpu.VMEM((stages, 2 * width, width), F32),
+            pltpu.VMEM((stages + 1, 2 * width, width), F32),
             pltpu.VMEM((stages, width, width), F32),
             pltpu.VMEM((stages + 1, width, width), F32),
             pltpu.VMEM((stages, width, width), F32),
             pltpu.VMEM((stages + 1, width, width), F32),
             pltpu.VMEM((2, width, 2 * width), F32),
             pltpu.VMEM((6, width, width), F32),
-            pltpu.VMEM((block, width), BF16),
+            pltpu.VMEM((devices, 2 * width, block), BF16),
+            pltpu.VMEM((devices, cells, block), BF16),
+            pltpu.VMEM((cells, width), BF16),
+            pltpu.VMEM((cells, profiles), BF16),
+            pltpu.VMEM((cells, width), F32),
+            pltpu.VMEM((2 * width, cells), BF16),
+            pltpu.VMEM((width, width), F32),
+            dma((devices // 2,)), dma((devices // 2,)),
             dma((stages, CHUNKS)), dma((stages, CHUNKS)),
         ]
-        + [dma((stages,))] * 6
-        + [dma],
+        + [dma((stages,))] * 8,
         compiler_params=pltpu.CompilerParams(
             collective_id=0, has_side_effects=True, vmem_limit_bytes=VMEM_LIMIT
         ),
-    )(ly_parts, gram_u, gram_s, cell_factor, k, sched_factor)
+    )(
+        cell_factor, core_matrix, rate_table, cell_well.reshape(1, cells),
+        sched_factor.reshape(devices, block, width),
+        sched_profile.reshape(devices, 1, block),
+    )
 
 
 def solution(mesh):

time: 126 us -> 103 us (0.82)
  Pallas kernels: 119 us -> 98.3 us
  local copies, waits for them, and re-layouts: 5.8 us -> 3.84 us
    pallas_call x1 -> x0, Pallas kernels: 30.8 us -> none  [local(): pl.pallas_call(functools.partial(tile_kernel, devices, PANEL_SCALE / n_sc...]
    pallas_call x1, Pallas kernels: 88 us -> 98.3 us  [local(): pl.pallas_call(functools.partial(comm_kernel, devices, n_cells, n_sched),...]
    unnamed x3 -> x7, local copies, waits for them, and re-layouts: 5.8 us -> 3.84 us
where the time goes in v2:
time: 103 us
  Pallas kernels  98.3 us (95%)
  local copies, waits for them, and re-layouts  3.84 us (4%)
    pallas_call x1, Pallas kernels, local(): pl.pallas_call(functools.partial(comm_kernel, devices, n_cells, n_sched),...  98.3 us
    unnamed x7, local copies, waits for them, and re-layouts  3.84 us

profile of v2, /device:TPU:0, one launch (start us, length us, event | category | flops | bytes accessed | tf_op | source)
XLA Modules:
  0.0 102.8 jit_solution(17995355584895900256)
XLA Ops:
  0.6 98.3 %shard_map.85 = (f32[1024,256]{1,0:T(8,128)}, f32[512,256]{1,0:T(8,128)}, f32[256,256]{1,0:T(8,128)}) custom-call(bf16[1024,128]{1,0:T(8,128)(2,1)} %cell_ref.1, f32[128,128]{1,0:T(8,128)} %core_matrix_ref.1, bf16[64,128]{1,0:T(8,128)(2,1)} %rate_ref.1, s32[1,1024]{1,0:T(1,128)} %bitcast.5, bf16[16,512,128]{2,1,0:T(8,128)(2,1)} %bitcast.3, s32[16,1,512]{2,1,0:T(1,128)} %bitcast.4), custom_call_target="tpu_custom_call" | custom-call | tf_op jit(solution)/shard_map/pallas_call | solution.py:340
  99.0 0.0 copy-start
  99.0 0.0 copy-start.1
  99.0 2.3 %copy.12 = f32[1024,256]{1,0:T(8,128)} copy(f32[1024,256]{1,0:T(8,128)} %get-tuple-element.6) | data formatting | bytes 2097152
  101.3 0.0 copy-done
  101.3 0.8 copy.13
  102.1 0.0 copy-done.1
  102.1 0.7 copy.14
Async XLA Ops:
  99.0 2.4 %copy-start = (f32[512,256]{1,0:T(8,128)S(1)}, f32[512,256]{1,0:T(8,128)}, u32[]{:S(2)}) copy-start(f32[512,256]{1,0:T(8,128)} %get-tuple-element.7) | copy-start | bytes 1572868
  99.0 3.1 %copy-start.1 = (f32[256,256]{1,0:T(8,128)S(1)}, f32[256,256]{1,0:T(8,128)}, u32[]{:S(2)}) copy-start(f32[256,256]{1,0:T(8,128)} %get-tuple-element.8) | copy-start | bytes 786436

commit v3 on v2

--- a/solution.py
+++ b/solution.py
@@ -25,7 +25,7 @@
 
 def bit_order(devices):
     bits = devices.bit_length() - 1
-    return [b for b in (0, 1) if b < bits] + list(range(bits - 1, 1, -1))
+    return list(range(bits))
 
 
 def owner_of(place, devices):
@@ -326,6 +326,12 @@
             hop(name, s).wait_send()
 
 
+def hand_on(*refs):
+    half = len(refs) // 2
+    for source, target in zip(refs[:half], refs[half:]):
+        target[...] = source[...]
+
+
 def local(cell_factor, sched_factor, core_matrix, rate_table, cell_well, sched_profile):
     cells, width = cell_factor.shape
     n_sched = sched_factor.shape[0]
@@ -337,7 +343,7 @@
     sds = jax.ShapeDtypeStruct
     vmem = pl.BlockSpec(memory_space=pltpu.VMEM)
     dma = pltpu.SemaphoreType.DMA
-    return pl.pallas_call(
+    outs = pl.pallas_call(
         functools.partial(comm_kernel, devices, n_cells, n_sched),
         in_specs=[vmem] * 6,
         out_specs=[vmem] * 3,
@@ -380,6 +386,14 @@
         sched_factor.reshape(devices, block, width),
         sched_profile.reshape(devices, 1, block),
     )
+    return tuple(
+        pl.pallas_call(
+            hand_on,
+            in_specs=[vmem] * 3,
+            out_specs=[vmem] * 3,
+            out_shape=[sds(o.shape, o.dtype) for o in outs],
+        )(*outs)
+    )
 
 
 def solution(mesh):

time: 103 us -> 101 us (0.981)
  local copies, waits for them, and re-layouts: 3.84 us -> 0 us
  Pallas kernels: 98.3 us -> 100 us
    unnamed x7 -> x0, local copies, waits for them, and re-layouts: 3.84 us -> none
    pallas_call x0 -> x1, Pallas kernels: none -> 2.68 us  [local(): pl.pallas_call(hand_on, in_specs=[vmem] * 3, out_specs=[vmem] * 3, out_sh...]
where the time goes in v3:
time: 101 us
  Pallas kernels  100 us (99%)
    pallas_call x1, Pallas kernels, local(): pl.pallas_call(functools.partial(comm_kernel, devices, n_cells, n_sched),...  97.5 us
    pallas_call x1, Pallas kernels, local(): pl.pallas_call(hand_on, in_specs=[vmem] * 3, out_specs=[vmem] * 3, out_sh...  2.68 us

profile of v3, /device:TPU:0, one launch (start us, length us, event | category | flops | bytes accessed | tf_op | source)
XLA Modules:
  0.0 100.9 jit_solution(8513949988402840078)
XLA Ops:
  0.6 97.5 %shard_map.85 = (f32[1024,256]{1,0:T(8,128)}, f32[512,256]{1,0:T(8,128)}, f32[256,256]{1,0:T(8,128)}) custom-call(bf16[1024,128]{1,0:T(8,128)(2,1)} %cell_ref.1, f32[128,128]{1,0:T(8,128)} %core_matrix_ref.1, bf16[64,128]{1,0:T(8,128)(2,1)} %rate_ref.1, s32[1,1024]{1,0:T(1,128)} %bitcast.5, bf16[16,512,128]{2,1,0:T(8,128)(2,1)} %bitcast.3, s32[16,1,512]{2,1,0:T(1,128)} %bitcast.4), custom_call_target="tpu_custom_call" | custom-call | tf_op jit(solution)/shard_map/pallas_call | solution.py:346
  98.2 2.7 %shard_map.86 = (f32[1024,256]{1,0:T(8,128)}, f32[512,256]{1,0:T(8,128)}, f32[256,256]{1,0:T(8,128)}) custom-call(f32[1024,256]{1,0:T(8,128)} %get-tuple-element.6.refs_0_, f32[512,256]{1,0:T(8,128)} %get-tuple-element.7.refs_1_, f32[256,256]{1,0:T(8,128)} %get-tuple-element.8.refs_2_), custom_call_target="tpu_custom_call" | custom-call | tf_op jit(solution)/shard_map/pallas_call | solution.py:390
